TPU v7x, 512 devices: a whole 4x4x16 slice. The times are simulated.
512 devices in a mesh: tm: 8 (over x, core), dp: 64 (over z, y).
Axes of the slice: x: 4, y: 4, z: 16, core: 2. Of those that a mesh axis runs over, the one named last changes fastest.
Arguments:
- edge_feat: bfloat16 [8, 8192, 186], P('tm', 'dp'), may hold values from -6 to 6
- endpoint_slots: int32 [8, 2, 8192], P('tm', None, 'dp'), may hold values from 0 to 2047, as said below
- neighbor_slots: int32 [8, 20, 8192], P('tm', None, 'dp'), may hold values from 0 to 2047, as said below
- neighbor_gap: int32 [8, 20, 8192], P('tm', None, 'dp'), may hold values from 0 to 999
- score_grad: float32 [8, 8192], P('tm', 'dp'), may hold values from -1.5 to 1.5
- node_list: int32 [8, 64, 2048], P('tm', 'dp'), may hold values from 0 to 128, as said below
- memory0: float32 [8192, 256], P('dp'), may hold values from -6 to 6
- msg_weight: bfloat16 [186, 256], replicated, may hold values from -0.4375 to 0.4375
- gate_weight: bfloat16 [256, 512], replicated, may hold values from -0.375 to 0.375
- gate_bias: float32 [512], replicated, may hold values from -4 to 4
- omega: float32 [256], replicated, may hold values from 0.001 to 1
- attn_weights: bfloat16 [4, 256, 256], replicated, may hold values from -0.375 to 0.375
- pred_weights: bfloat16 [2, 256, 256], replicated, may hold values from -0.375 to 0.375
- pred_out: float32 [256], replicated, may hold values from -0.375 to 0.375
Outputs:
- scores: float32 [8, 8192], P('tm', 'dp')
- new_memory: float32 [8, 8192, 256], P('tm', 'dp')
- grad_out_proj: float32 [256, 256], replicated
- grad_pred: float32 [2, 256, 256], replicated
Inputs may be any that keep to these rules, and one draw needn't show every extreme that they name: `node_list`: each block of 32 slots (one device's requests to one owner) holds distinct rows first and 128 in the empty slots after them; every block holds at least one row; in each mini-batch some owner's block is full from every device. `endpoint_slots`: every slot points at a non-empty entry of its device's node list. `neighbor_slots`: every slot points at a non-empty entry of its device's node list.
All inputs are finite; a program needn't handle non-finite values.
Results may differ from a plain program's by a relative error of at most 0.017.
Values may be sent and summed in bfloat16 or wider, within the bound.
No kernel may reach another device: no remote copies, remote signals or barrier semaphores. Data moves between devices by JAX's collectives and lax.ppermute only.
A program may use at most 64 MiB of HBM per device.

v0:
```python
import math
import jax
import jax.numpy as jnp
from jax import lax
from jax.sharding import PartitionSpec as P

HEADS = 2


def shifted(value, axis, steps):
    count = lax.axis_size(axis)
    initial, last = (max(0, -steps), min(count, count - steps))
    return lax.ppermute(value, axis, [(source, source + steps) for source in range(initial, last)])


def local_step(
    slot_rows,
    end_slots,
    near_slots,
    near_gaps,
    cot_rows,
    omega,
    attn_weights,
    pred_weights,
    pred_out,
):
    feat_width = slot_rows.shape[1]
    events = end_slots.shape[1]
    near_count = near_slots.shape[0] // 2
    head_dim = feat_width // HEADS
    self_rows = jnp.take(slot_rows, end_slots, axis=0)
    near_rows = jnp.take(slot_rows, near_slots, axis=0).reshape(2, near_count, events, feat_width)
    phases = near_gaps.reshape(2, near_count, events).astype(jnp.float32)[..., None] * omega
    near_feat = (near_rows.astype(jnp.float32) + jnp.cos(phases)).astype(jnp.bfloat16)
    query_proj = jnp.einsum(
        "pea,ab->peb", self_rows, attn_weights[0], preferred_element_type=jnp.float32
    )
    key_proj = jnp.einsum(
        "pkea,ab->pkeb", near_feat, attn_weights[1], preferred_element_type=jnp.float32
    )
    value_proj = jnp.einsum(
        "pkea,ab->pkeb", near_feat, attn_weights[2], preferred_element_type=jnp.float32
    )
    query_heads = query_proj.reshape(2, 1, events, HEADS, head_dim)
    key_heads = key_proj.reshape(2, near_count, events, HEADS, head_dim)
    value_heads = value_proj.reshape(2, near_count, events, HEADS, head_dim)
    att_logits = jnp.sum(query_heads * key_heads, axis=-1) / math.sqrt(head_dim)
    weights_att = jax.nn.softmax(att_logits, axis=1)
    mixed_heads = (
        jnp.sum(weights_att[..., None] * value_heads, axis=1)
        .reshape(2, events, feat_width)
        .astype(jnp.bfloat16)
    )
    state_full = self_rows.astype(jnp.float32) + jnp.einsum(
        "pea,ab->peb", mixed_heads, attn_weights[3], preferred_element_type=jnp.float32
    )
    state_bf = state_full.astype(jnp.bfloat16)
    pre_pred = jnp.dot(state_bf[0], pred_weights[0], preferred_element_type=jnp.float32) + jnp.dot(
        state_bf[1], pred_weights[1], preferred_element_type=jnp.float32
    )
    sigmoid_pre = jax.nn.sigmoid(pre_pred)
    logit_out = jnp.sum(pre_pred * sigmoid_pre * pred_out, axis=-1)
    grad_pre = (
        cot_rows[:, None] * pred_out * (sigmoid_pre * (1.0 + pre_pred * (1.0 - sigmoid_pre)))
    ).astype(jnp.bfloat16)
    grad_first = jnp.einsum("ea,eb->ab", state_bf[0], grad_pre, preferred_element_type=jnp.float32)
    grad_second = jnp.einsum("ea,eb->ab", state_bf[1], grad_pre, preferred_element_type=jnp.float32)
    grad_state = jnp.einsum(
        "eb,pab->pea", grad_pre, pred_weights, preferred_element_type=jnp.float32
    ).astype(jnp.bfloat16)
    grad_out_proj = jnp.einsum(
        "pea,peb->ab", mixed_heads, grad_state, preferred_element_type=jnp.float32
    )
    return (logit_out, grad_out_proj, jnp.stack([grad_first, grad_second]))


def per_device(
    edge_feat,
    endpoint_slots,
    neighbor_slots,
    neighbor_gap,
    score_grad,
    node_list,
    memory0,
    msg_weight,
    gate_weight,
    gate_bias,
    omega,
    attn_weights,
    pred_weights,
    pred_out,
):
    groups = lax.axis_size("dp")
    node_dev, feat_width = memory0.shape
    list_len = node_list.shape[2]
    per_owner = list_len // groups
    requests = node_list[0, 0].reshape(groups, per_owner)
    wanted = lax.all_to_all(requests, "dp", split_axis=0, concat_axis=0, tiled=True)
    message = jnp.dot(edge_feat[0], msg_weight, preferred_element_type=jnp.float32).astype(
        jnp.bfloat16
    )
    message_wide = message.astype(jnp.float32)
    end_slots = endpoint_slots[0]
    flat_ends = end_slots.reshape(-1)
    slot_sums = (
        jnp.zeros((list_len, feat_width), jnp.float32)
        .at[flat_ends]
        .add(jnp.concatenate([message_wide, message_wide]))
    )
    slot_tally = jnp.zeros((list_len,), jnp.float32).at[flat_ends].add(1.0)
    got_sums, got_tally = (
        lax.all_to_all(
            slot_sums.reshape(groups, per_owner, feat_width),
            "dp",
            split_axis=0,
            concat_axis=0,
            tiled=True,
        ),
        lax.all_to_all(
            slot_tally.reshape(groups, per_owner), "dp", split_axis=0, concat_axis=0, tiled=True
        ),
    )
    picker = (wanted.reshape(-1)[:, None] == jnp.arange(node_dev)[None, :]).astype(jnp.bfloat16)
    flat_sums = got_sums.reshape(-1, feat_width)
    sums_high = flat_sums.astype(jnp.bfloat16)
    sums_low = (flat_sums - sums_high.astype(jnp.float32)).astype(jnp.bfloat16)
    totals = jnp.einsum(
        "sn,sd->nd", picker, sums_high, preferred_element_type=jnp.float32
    ) + jnp.einsum("sn,sd->nd", picker, sums_low, preferred_element_type=jnp.float32)
    counts = jnp.dot(
        got_tally.reshape(-1), picker.astype(jnp.float32), precision=lax.Precision.HIGHEST
    )
    touched = (counts > 0.5).astype(jnp.float32)
    mean_msg = (totals / jnp.maximum(counts, 1.0)[:, None]).astype(jnp.bfloat16)
    pre_gate = jnp.dot(mean_msg, gate_weight, preferred_element_type=jnp.float32) + gate_bias
    update = jax.nn.sigmoid(pre_gate[:, :feat_width]) * touched[:, None]
    candidate = jnp.tanh(pre_gate[:, feat_width:])
    decay_rate = 1.0 - update
    inject = update * candidate
    section_index = lax.axis_index("tm")
    before = memory0
    for relay_step in range(lax.axis_size("tm") - 1):
        moved_state = shifted((decay_rate * before + inject).astype(jnp.bfloat16), "tm", 1).astype(
            jnp.float32
        )
        before = jnp.where(section_index == 0, memory0, moved_state)
    new_memory = decay_rate * before + inject
    memory_bf = before.astype(jnp.bfloat16)
    full_table = lax.all_gather(memory_bf, "dp", axis=0, tiled=True)
    owner_of = jnp.arange(list_len, dtype=jnp.int32) // per_owner
    global_row = owner_of * node_dev + jnp.minimum(node_list[0, 0], node_dev - 1)
    slot_rows = jnp.take(full_table, global_row, axis=0)
    logit_out, grad_out, grad_pair = local_step(
        slot_rows,
        end_slots,
        neighbor_slots[0],
        neighbor_gap[0],
        score_grad[0],
        omega,
        attn_weights,
        pred_weights,
        pred_out,
    )
    grad_out, grad_pair = lax.psum((grad_out, grad_pair), ("tm", "dp"))
    return (logit_out[None, :], new_memory[None], grad_out, grad_pair)


def solution(mesh):
    in_specs = (
        P("tm", "dp", None),
        P("tm", None, "dp"),
        P("tm", None, "dp"),
        P("tm", None, "dp"),
        P("tm", "dp"),
        P("tm", "dp", None),
        P("dp", None),
        P(),
        P(),
        P(),
        P(),
        P(),
        P(),
        P(),
    )
    out_specs = (P("tm", "dp"), P("tm", "dp", None), P(), P())
    return jax.shard_map(
        per_device, mesh=mesh, in_specs=in_specs, out_specs=out_specs, check_vma=False
    )
```

profile of v0, /device:TPU:2, one launch (start us, length us, event | category | flops | bytes accessed | tf_op | source)
XLA Modules:
  0.0 856.8 jit_solution(11601709572848172272)
XLA Ops:
  7.2 0.5 broadcast.325
  7.7 1.4 broadcast_minimum_fusion
  9.1 0.7 all_to_all.15
  9.8 18.7 %all-to-all-start = ((s32[64,1,32]{2,1,0:T(1,128)}), s32[64,1,32]{2,1,0:T(1,128)S(1)}, u32[]{:S(2)}, u32[]{:S(2)}) async-start(s32[64,1,32]{2,1,0:T(1,128)} %bitcast.2), calls=%async_computation | async-start | bytes 65536 | tf_op jit(solution)/shard_map/all_to_all | solution.py:98
  28.5 0.7 compare_select_fusion.4
  29.2 2.0 scatter_custom_fusion.1
  31.2 0.7 all_to_all.18
  31.8 11.2 %all-to-all-done = s32[64,1,32]{2,1,0:T(1,128)S(1)} async-done(((s32[64,1,32]{2,1,0:T(1,128)}), s32[64,1,32]{2,1,0:T(1,128)S(1)}, u32[]{:S(2)}, u32[]{:S(2)}) %all-to-all-start) | async-done | bytes 8224 | tf_op jit(solution)/shard_map/all_to_all | solution.py:98
  43.0 4.6 all-to-all-start.2
  47.6 1.1 convolution_convert_fusion.1
  48.7 3.4 scatter_custom_fusion
  52.1 10.2 %all-to-all-done.2 = f32[64,1,32]{2,1,0:T(1,128)S(1)} async-done(((f32[64,1,32]{2,1,0:T(1,128)}), f32[64,1,32]{2,1,0:T(1,128)S(1)}, u32[]{:S(2)}, u32[]{:S(2)}) %all-to-all-start.2) | async-done | bytes 8224 | tf_op jit(solution)/shard_map/all_to_all | solution.py:119
  62.3 4.9 all-to-all-start.1
  67.3 0.7 reduce.12
  68.1 0.5 broadcast.327
  68.6 0.7 reduce.13
  69.4 0.6 compare_convert_fusion
  70.0 95.7 %all-to-all-done.1 = f32[64,32,256]{2,1,0:T(8,128)S(1)} async-done(((f32[64,32,256]{2,1,0:T(8,128)}), f32[64,32,256]{2,1,0:T(8,128)S(1)}, u32[]{:S(2)}, u32[]{:S(2)}) %all-to-all-start.1) | async-done | bytes 2097184 | tf_op jit(solution)/shard_map/all_to_all | solution.py:112
  165.8 0.2 fusion
  166.0 0.8 fusion.7
  166.8 1.0 convolution_add_fusion.1
  167.9 0.1 add_convert_fusion.7
  168.0 2.1 collective-permute-start
  170.0 3.6 collective-permute-done
  173.8 1.9 collective-permute-start.1
  175.7 3.7 collective-permute-done.1
  179.5 2.1 collective-permute-start.2
  181.5 3.7 collective-permute-done.2
  185.3 1.9 collective-permute-start.3
  187.2 3.7 collective-permute-done.3
  191.0 1.9 collective-permute-start.4
  192.9 3.7 collective-permute-done.4
  196.6 0.1 add_convert_fusion.2
  196.7 1.9 collective-permute-start.5
  198.6 3.7 collective-permute-done.5
  202.3 1.9 collective-permute-start.6
  204.3 3.7 collective-permute-done.6
  207.9 0.6 fusion.30
  208.6 0.2 all-reduce.3.cloned.1.call-start
  208.9 0.1 copy.37
  209.0 0.8 copy.39
  209.8 0.8 copy.40
  210.7 136.2 %all-gather.2.cloned.1.call-done = bf16[8192,256]{1,0:T(8,128)(2,1)} async-done(((bf16[128,256]{1,0:T(8,128)(2,1)}), bf16[8192,256]{1,0:T(8,128)(2,1)}) %all-gather.2.cloned.1.call-update) | async-done | bytes 4194320 | tf_op jit(solution)/shard_map/all_gather | solution.py:149
  346.9 9.4 %gather_fusion = bf16[2048,256]{1,0:T(8,128)(2,1)S(1)} fusion(bf16[8192,256]{1,0:T(8,128)(2,1)} %all-gather.2.cloned.1.call-done, s32[2048]{0:T(1024)S(1)} %broadcast_clamp_fusion), kind=kCustom, calls=%fused_computation | custom fusion | bytes 2105344 | tf_op jit(solution)/shard_map/jit(_take)/gather | solution.py:152
  356.3 0.4 broadcast_select_fusion
  356.7 7.6 gather_fusion.2
  364.3 1.2 gather_fusion.1
  365.5 0.3 fusion.21
  365.8 10.1 %add_convert_fusion = bf16[20,128,256]{2,1,0:T(8,128)(2,1)S(1)} fusion(f32[256]{0:T(256)S(1)} %copy-done.10, f32[20,128]{1,0:T(8,128)S(1)} %bitcast.137, bf16[20,128,256]{2,1,0:T(8,128)(2,1)S(1)} %bitcast.127, pred[20,128]{1,0:T(8,128)(4,1)S(1)} %compare_and_fusion), kind=kLoop, calls=%fused_computation.7 | loop fusion | flops 3276800 | bytes 2635264 | tf_op jit(solution)/shard_map/convert_element_type | solution.py:34
  375.9 0.6 multiply_reduce_fusion.1
  376.6 0.2 copy-done.3
  376.8 1.1 multiply_reduce_fusion
  377.9 0.1 copy.41
  378.1 1.1 fusion.1
  379.2 0.2 fusion.24
  379.4 0.8 multiply_reduce_fusion.2
  380.2 0.2 convolution_bitcast_fusion.1
  380.4 0.2 convolution_bitcast_fusion
  380.7 1.1 convolution_bitcast_fusion.2
  381.8 0.8 pad_maximum_fusion
  382.6 0.7 add_bitcast_fusion
  383.4 463.0 %all-reduce.3.cloned.1.call-done = (f32[256,256]{1,0:T(8,128)}, f32[2,256,256]{2,1,0:T(8,128)}) async-done(((f32[256,256]{1,0:T(8,128)}, f32[2,256,256]{2,1,0:T(8,128)}), (f32[256,256]{1,0:T(8,128)}, f32[2,256,256]{2,1,0:T(8,128)})) %all-reduce.3.cloned.1.call-update) | async-done | bytes 786448 | tf_op jit(solution)/shard_map/psum | solution.py:164
  846.4 1.7 copy.58
  848.1 1.9 copy.59
  (54 shorter events, 1.0 us)
Async XLA Ops:
  7.2 159.7 %copy-start = (bf16[256,512]{1,0:T(8,128)(2,1)S(1)}, bf16[256,512]{1,0:T(8,128)(2,1)}, u32[]{:S(2)}) copy-start(bf16[256,512]{1,0:T(8,128)(2,1)} %param.22) | copy-start | bytes 786436
  9.8 33.3 %all-to-all-start = ((s32[64,1,32]{2,1,0:T(1,128)}), s32[64,1,32]{2,1,0:T(1,128)S(1)}, u32[]{:S(2)}, u32[]{:S(2)}) async-start(s32[64,1,32]{2,1,0:T(1,128)} %bitcast.2), calls=%async_computation | async-start | bytes 65536 | tf_op jit(solution)/shard_map/all_to_all | solution.py:98
  43.0 19.3 %all-to-all-start.2 = ((f32[64,1,32]{2,1,0:T(1,128)}), f32[64,1,32]{2,1,0:T(1,128)S(1)}, u32[]{:S(2)}, u32[]{:S(2)}) async-start(f32[64,1,32]{2,1,0:T(1,128)} %bitcast.8), calls=%async_computation.2 | async-start | bytes 65536 | tf_op jit(solution)/shard_map/all_to_all | solution.py:119
  62.3 103.4 %all-to-all-start.1 = ((f32[64,32,256]{2,1,0:T(8,128)}), f32[64,32,256]{2,1,0:T(8,128)S(1)}, u32[]{:S(2)}, u32[]{:S(2)}) async-start(f32[64,32,256]{2,1,0:T(8,128)} %bitcast.6), calls=%async_computation.1 | async-start | bytes 4194304 | tf_op jit(solution)/shard_map/all_to_all | solution.py:112
  67.2 279.7 %all-gather.2.cloned.1.call-start = ((), (), s32[]{:S(2)}) async-start(), calls=%async_computation.3 | async-start | bytes 4259840 | tf_op jit(solution)/shard_map/all_gather | solution.py:149
  70.0 96.8 %copy-start.11 = (f32[512]{0:T(512)S(1)}, f32[512]{0:T(512)}, u32[]{:S(2)}) copy-start(f32[512]{0:T(512)} %param.23) | copy-start | bytes 6148
  166.0 1.8 copy-start.1
  167.8 41.0 %copy-start.8 = (s32[1,20,128]{2,0,1:T(1,128)S(1)}, s32[1,20,128]{2,0,1:T(1,128)}, u32[]{:S(2)}) copy-start(s32[1,20,128]{2,0,1:T(1,128)} %param.17) | copy-start | bytes 30724
  167.8 41.0 %copy-start.2 = (bf16[4,256,256]{2,1,0:T(8,128)(2,1)S(1)}, bf16[4,256,256]{2,1,0:T(8,128)(2,1)}, u32[]{:S(2)}) copy-start(bf16[4,256,256]{2,1,0:T(8,128)(2,1)} %param.25) | copy-start | bytes 1572868
  168.0 5.7 collective-permute-start
  173.8 5.6 collective-permute-start.1
  179.4 31.1 %copy-start.9 = (s32[1,2,128]{2,1,0:T(2,128)S(1)}, s32[1,2,128]{2,1,0:T(2,128)}, u32[]{:S(2)}) copy-start(s32[1,2,128]{2,1,0:T(2,128)} %param.15) | copy-start | bytes 3076
  179.5 31.1 %copy-start.6 = (s32[1,20,128]{2,0,1:T(1,128)S(1)}, s32[1,20,128]{2,0,1:T(1,128)}, u32[]{:S(2)}) copy-start(s32[1,20,128]{2,0,1:T(1,128)} %param.16) | copy-start | bytes 30724
  179.5 31.2 %copy-start.7 = (s32[1,1,2048]{2,1,0:T(1,128)S(1)}, s32[1,1,2048]{2,1,0:T(1,128)}, u32[]{:S(2)}) copy-start(s32[1,1,2048]{2,1,0:T(1,128)} %param.19) | copy-start | bytes 24580
  179.5 5.7 collective-permute-start.2
  185.3 5.6 collective-permute-start.3
  191.0 5.6 collective-permute-start.4
  196.7 5.6 collective-permute-start.5
  202.3 5.6 collective-permute-start.6
  208.6 637.8 %all-reduce.3.cloned.1.call-start = ((), (), s32[]{:S(2)}) async-start(), calls=%async_computation.4 | async-start | bytes 1572864 | tf_op jit(solution)/shard_map/psum | solution.py:164
  356.7 9.0 %copy-start.10 = (f32[256]{0:T(256)S(1)}, f32[256]{0:T(256)}, u32[]{:S(2)}) copy-start(f32[256]{0:T(256)} %param.24) | copy-start | bytes 3076
  365.5 10.5 %copy-start.4 = (bf16[256,256]{1,0:T(8,128)(2,1)S(1)}, bf16[256,256]{1,0:T(8,128)(2,1)}, u32[]{:S(2)}) copy-start(bf16[256,256]{1,0:T(8,128)(2,1)} %copy.39) | copy-start | bytes 393220
  375.9 0.9 copy-start.3
  376.5 2.7 copy-start.5
  376.8 2.6 copy-start.12
  376.8 3.4 copy-start.13
Sparse Core Ops, SparseCore 0:
  208.7 138.1 all-gather.1
  382.8 463.6 all-reduce.2
where the time goes:
time: 858 us; the launch traced here: 857 us
  waiting for transfers between devices  742 us (86%)
  starting transfers between devices  42.2 us (5%)
  local copies, waits for them, and re-layouts  26.3 us (3%)
  other arithmetic  22.7 us (3%)
  between operations  14.6 us (2%)
  matrix products  9.08 us (1%)
    psum x1, waiting for transfers between devices, per_device(): grad_out, grad_pair = lax.psum((grad_out, grad_pair), ('tm', 'dp'))  463 us
    all_gather x1, waiting for transfers between devices, per_device(): full_table = lax.all_gather(memory_bf, 'dp', axis=0, tiled=True)  136 us
    all_to_all x1, waiting for transfers between devices, per_device(): lax.all_to_all(slot_sums.reshape(groups, per_owner, feat_width), 'dp', sp...  95.7 us
    ppermute x7, waiting for transfers between devices, shifted(): lax.ppermute(value, axis, [(source, source + steps) for source in range(i...  25.6 us
    all_to_all x1, starting transfers between devices, per_device(): lax.all_to_all(requests, 'dp', split_axis=0, concat_axis=0, tiled=True)  18.7 us
  transfers between devices with their start and end apart: 12, of which 12 were waited for; matrix products, arithmetic and copies ran while one was open for 1% of the time, Pallas kernels for 0%

commit v1 on v0

--- a/solution.py
+++ b/solution.py
@@ -146,7 +146,10 @@
         before = jnp.where(section_index == 0, memory0, moved_state)
     new_memory = decay_rate * before + inject
     memory_bf = before.astype(jnp.bfloat16)
-    full_table = lax.all_gather(memory_bf, "dp", axis=0, tiled=True)
+    count_2 = lax.axis_size("dp")
+    parts = jnp.stack([memory_bf for _ in range(count_2)])
+    parts = lax.all_to_all(parts, "dp", split_axis=0, concat_axis=0)
+    full_table = jnp.concatenate(parts, axis=0)
     owner_of = jnp.arange(list_len, dtype=jnp.int32) // per_owner
     global_row = owner_of * node_dev + jnp.minimum(node_list[0, 0], node_dev - 1)
     slot_rows = jnp.take(full_table, global_row, axis=0)

time: 858 us -> 913 us (1.064)
  waiting for transfers between devices: 742 us -> 789 us
    all_to_all x0 -> x1, waiting for transfers between devices: none -> 187 us  [per_device(): parts = lax.all_to_all(parts, 'dp', split_axis=0, concat_axis=0)]
    all_gather x1 -> x0, waiting for transfers between devices: 136 us -> none  [per_device(): full_table = lax.all_gather(memory_bf, 'dp', axis=0, tiled=True)]
where the time goes in v1:
time: 913 us; the launch traced here: 912 us
  waiting for transfers between devices  789 us (86%)
  starting transfers between devices  48.1 us (5%)
  local copies, waits for them, and re-layouts  28.7 us (3%)
  other arithmetic  22.1 us (2%)
  between operations  14.6 us (2%)
    psum x1, waiting for transfers between devices, per_device(): grad_out, grad_pair = lax.psum((grad_out, grad_pair), ('tm', 'dp'))  459 us
    all_to_all x1, waiting for transfers between devices, per_device(): parts = lax.all_to_all(parts, 'dp', split_axis=0, concat_axis=0)  187 us
    all_to_all x1, waiting for transfers between devices, per_device(): lax.all_to_all(slot_sums.reshape(groups, per_owner, feat_width), 'dp', sp...  95.8 us
    ppermute x7, waiting for transfers between devices, shifted(): lax.ppermute(value, axis, [(source, source + steps) for source in range(i...  25.6 us
    all_to_all x1, starting transfers between devices, per_device(): lax.all_to_all(requests, 'dp', split_axis=0, concat_axis=0, tiled=True)  18.7 us
  transfers between devices with their start and end apart: 12, of which 12 were waited for; matrix products, arithmetic and copies ran while one was open for 1% of the time, Pallas kernels for 0%

profile of v1, /device:TPU:2, one launch (start us, length us, event | category | flops | bytes accessed | tf_op | source)
XLA Modules:
  0.0 912.0 jit_solution(10934504841420755870)
XLA Ops:
  7.2 0.5 broadcast.327
  7.7 1.4 broadcast_minimum_fusion
  9.1 0.7 all_to_all.18
  9.8 18.7 %all-to-all-start = ((s32[64,1,32]{2,1,0:T(1,128)}), s32[64,1,32]{2,1,0:T(1,128)S(1)}, u32[]{:S(2)}, u32[]{:S(2)}) async-start(s32[64,1,32]{2,1,0:T(1,128)} %bitcast.2), calls=%async_computation | async-start | bytes 65536 | tf_op jit(solution)/shard_map/all_to_all | solution.py:98
  28.5 0.7 compare_select_fusion.4
  29.2 2.0 scatter_custom_fusion.1
  31.2 0.7 all_to_all.21
  31.8 11.2 %all-to-all-done = s32[64,1,32]{2,1,0:T(1,128)S(1)} async-done(((s32[64,1,32]{2,1,0:T(1,128)}), s32[64,1,32]{2,1,0:T(1,128)S(1)}, u32[]{:S(2)}, u32[]{:S(2)}) %all-to-all-start) | async-done | bytes 8224 | tf_op jit(solution)/shard_map/all_to_all | solution.py:98
  43.0 4.6 all-to-all-start.2
  47.6 1.1 convolution_convert_fusion.1
  48.7 3.4 scatter_custom_fusion
  52.1 10.2 %all-to-all-done.2 = f32[64,1,32]{2,1,0:T(1,128)S(1)} async-done(((f32[64,1,32]{2,1,0:T(1,128)}), f32[64,1,32]{2,1,0:T(1,128)S(1)}, u32[]{:S(2)}, u32[]{:S(2)}) %all-to-all-start.2) | async-done | bytes 8224 | tf_op jit(solution)/shard_map/all_to_all | solution.py:119
  62.3 4.9 all-to-all-start.1
  67.2 0.7 reduce.12
  68.0 0.5 broadcast.329
  68.5 0.7 reduce.13
  69.4 0.6 compare_convert_fusion
  70.0 95.8 %all-to-all-done.1 = f32[64,32,256]{2,1,0:T(8,128)S(1)} async-done(((f32[64,32,256]{2,1,0:T(8,128)}), f32[64,32,256]{2,1,0:T(8,128)S(1)}, u32[]{:S(2)}, u32[]{:S(2)}) %all-to-all-start.1) | async-done | bytes 2097184 | tf_op jit(solution)/shard_map/all_to_all | solution.py:112
  165.7 0.2 fusion
  166.0 0.8 fusion.7
  166.8 1.0 convolution_add_fusion.1
  167.8 0.1 add_convert_fusion.7
  167.9 1.9 collective-permute-start
  169.9 3.6 collective-permute-done
  173.6 1.9 collective-permute-start.1
  175.5 3.7 collective-permute-done.1
  179.3 1.9 collective-permute-start.2
  181.2 3.7 collective-permute-done.2
  185.0 1.9 collective-permute-start.3
  186.9 3.7 collective-permute-done.3
  190.6 1.9 collective-permute-start.4
  192.6 3.7 collective-permute-done.4
  196.3 1.9 collective-permute-start.5
  198.2 3.7 collective-permute-done.5
  202.0 1.9 collective-permute-start.6
  203.9 3.7 collective-permute-done.6
  207.6 2.5 stack.8
  210.1 6.2 all-to-all-start.3
  216.3 0.2 all-reduce.3.cloned.1.call-start
  216.7 0.1 copy.37
  216.8 0.8 copy.39
  217.5 0.8 copy.40
  218.5 187.2 %all-to-all-done.3 = bf16[64,128,256]{2,1,0:T(8,128)(2,1)} async-done(((bf16[64,128,256]{2,1,0:T(8,128)(2,1)}), bf16[64,128,256]{2,1,0:T(8,128)(2,1)}, u32[]{:S(2)}, u32[]{:S(2)}) %all-to-all-start.3) | async-done | bytes 4194336 | tf_op jit(solution)/shard_map/all_to_all | solution.py:151
  405.7 9.4 %gather_fusion = bf16[2048,256]{1,0:T(8,128)(2,1)S(1)} fusion(bf16[8192,256]{1,0:T(8,128)(2,1)} %bitcast.10, s32[2048]{0:T(1024)S(1)} %broadcast_clamp_fusion), kind=kCustom, calls=%fused_computation | custom fusion | bytes 2105344 | tf_op jit(solution)/shard_map/jit(_take)/gather | solution.py:155
  415.1 0.4 broadcast_select_fusion
  415.6 7.6 gather_fusion.2
  423.1 1.2 gather_fusion.1
  424.3 0.3 fusion.21
  424.6 10.1 %add_convert_fusion = bf16[20,128,256]{2,1,0:T(8,128)(2,1)S(1)} fusion(f32[256]{0:T(256)S(1)} %copy-done.10, f32[20,128]{1,0:T(8,128)S(1)} %bitcast.138, bf16[20,128,256]{2,1,0:T(8,128)(2,1)S(1)} %bitcast.128, pred[20,128]{1,0:T(8,128)(4,1)S(1)} %compare_and_fusion), kind=kLoop, calls=%fused_computation.7 | loop fusion | flops 3276800 | bytes 2635264 | tf_op jit(solution)/shard_map/convert_element_type | solution.py:34
  434.7 0.6 multiply_reduce_fusion.1
  435.4 0.2 copy-done.3
  435.6 1.1 multiply_reduce_fusion
  436.7 0.1 copy.41
  436.9 1.1 fusion.1
  438.0 0.2 fusion.24
  438.2 0.8 multiply_reduce_fusion.2
  439.0 0.2 convolution_bitcast_fusion.1
  439.2 0.2 convolution_bitcast_fusion
  439.5 1.1 convolution_bitcast_fusion.2
  440.6 0.8 pad_maximum_fusion
  441.4 0.7 add_bitcast_fusion
  442.2 459.4 %all-reduce.3.cloned.1.call-done = (f32[256,256]{1,0:T(8,128)}, f32[2,256,256]{2,1,0:T(8,128)}) async-done(((f32[256,256]{1,0:T(8,128)}, f32[2,256,256]{2,1,0:T(8,128)}), (f32[256,256]{1,0:T(8,128)}, f32[2,256,256]{2,1,0:T(8,128)})) %all-reduce.3.cloned.1.call-update) | async-done | bytes 786448 | tf_op jit(solution)/shard_map/psum | solution.py:167
  901.6 1.7 copy.58
  903.3 1.9 copy.59
  (54 shorter events, 1.0 us)
Async XLA Ops:
  7.2 159.6 %copy-start = (bf16[256,512]{1,0:T(8,128)(2,1)S(1)}, bf16[256,512]{1,0:T(8,128)(2,1)}, u32[]{:S(2)}) copy-start(bf16[256,512]{1,0:T(8,128)(2,1)} %param.22) | copy-start | bytes 786436
  9.8 33.3 %all-to-all-start = ((s32[64,1,32]{2,1,0:T(1,128)}), s32[64,1,32]{2,1,0:T(1,128)S(1)}, u32[]{:S(2)}, u32[]{:S(2)}) async-start(s32[64,1,32]{2,1,0:T(1,128)} %bitcast.2), calls=%async_computation | async-start | bytes 65536 | tf_op jit(solution)/shard_map/all_to_all | solution.py:98
  43.0 19.3 %all-to-all-start.2 = ((f32[64,1,32]{2,1,0:T(1,128)}), f32[64,1,32]{2,1,0:T(1,128)S(1)}, u32[]{:S(2)}, u32[]{:S(2)}) async-start(f32[64,1,32]{2,1,0:T(1,128)} %bitcast.8), calls=%async_computation.2 | async-start | bytes 65536 | tf_op jit(solution)/shard_map/all_to_all | solution.py:119
  62.3 103.4 %all-to-all-start.1 = ((f32[64,32,256]{2,1,0:T(8,128)}), f32[64,32,256]{2,1,0:T(8,128)S(1)}, u32[]{:S(2)}, u32[]{:S(2)}) async-start(f32[64,32,256]{2,1,0:T(8,128)} %bitcast.6), calls=%async_computation.1 | async-start | bytes 4194304 | tf_op jit(solution)/shard_map/all_to_all | solution.py:112
  70.0 96.9 %copy-start.11 = (f32[512]{0:T(512)S(1)}, f32[512]{0:T(512)}, u32[]{:S(2)}) copy-start(f32[512]{0:T(512)} %param.23) | copy-start | bytes 6148
  166.0 1.8 copy-start.1
  167.9 5.6 collective-permute-start
  173.6 5.6 collective-permute-start.1
  179.3 5.6 collective-permute-start.2
  185.0 5.6 collective-permute-start.3
  190.6 5.6 collective-permute-start.4
  196.3 5.6 collective-permute-start.5
  202.0 5.6 collective-permute-start.6
  210.1 6.5 copy-start.8
  210.1 6.5 copy-start.2
  210.1 8.2 copy-start.9
  210.1 8.2 copy-start.6
  210.1 8.3 copy-start.7
  210.1 195.6 %all-to-all-start.3 = ((bf16[64,128,256]{2,1,0:T(8,128)(2,1)}), bf16[64,128,256]{2,1,0:T(8,128)(2,1)}, u32[]{:S(2)}, u32[]{:S(2)}) async-start(bf16[64,128,256]{2,1,0:T(8,128)(2,1)} %stack.8), calls=%async_computation.3 | async-start | bytes 8388608 | tf_op jit(solution)/shard_map/all_to_all | solution.py:151
  216.3 685.2 %all-reduce.3.cloned.1.call-start = ((), (), s32[]{:S(2)}) async-start(), calls=%async_computation.4 | async-start | bytes 1572864 | tf_op jit(solution)/shard_map/psum | solution.py:167
  415.5 9.0 copy-start.10
  424.3 10.5 %copy-start.4 = (bf16[256,256]{1,0:T(8,128)(2,1)S(1)}, bf16[256,256]{1,0:T(8,128)(2,1)}, u32[]{:S(2)}) copy-start(bf16[256,256]{1,0:T(8,128)(2,1)} %copy.39) | copy-start | bytes 393220
  434.7 0.9 copy-start.3
  435.3 2.7 copy-start.5
  435.6 2.5 copy-start.12
  435.6 3.4 copy-start.13
Sparse Core Ops, SparseCore 0:
  441.6 459.9 all-reduce.2
